TPU v7x, 512 devices: a whole 4x8x8 slice. The times are simulated.
512 devices in a mesh: loop: 16 (over x, y_lo, core), groups: 32 (over y_hi, z).
Axes of the slice: x: 4, y: 8 (y_hi: 4, y_lo: 2; y = y_hi * 2 + y_lo), z: 8, core: 2. Of those that a mesh axis runs over, the one named last changes fastest.
Arguments:
- states: bfloat16 [65536, 1024], P(('loop', 'groups')), may hold values from -64 to 64
- premises: bfloat16 [65536, 1024], P(('loop', 'groups')), may hold values from -1 to 1
- counts: int32 [16, 32], P('loop', 'groups'), may hold values from 64 to 128, as said below
- partner_mask: int32 [16], P('loop'), may hold values from 0 to 31, as said below
- send_rows: int32 [16, 32, 16], P('loop', 'groups'), may hold values from 0 to 63
- hard_idx: int32 [65536], P(('loop', 'groups')), may hold values from 0 to 15
Outputs:
- loss: float32 [], replicated
- grad_states: bfloat16 [65536, 1024], P(('loop', 'groups'))
- grad_premises: bfloat16 [65536, 1024], P(('loop', 'groups'))
Inputs may be any that keep to these rules, and one draw needn't show every extreme that they name: `counts`: at least 64 valid pairs on every device; some device has all slots valid. `partner_mask`: loop index 0 has the value 32 // 2.
All inputs are finite; a program needn't handle non-finite values.
Results may differ from a plain program's by a relative error of at most 0.0034.
Values may be sent and summed in bfloat16 or wider, within the bound.
A program may use at most 64 MiB of HBM per device.

v0:
```python
import jax
import jax.numpy as jnp
from jax import lax
from jax.sharding import PartitionSpec as P

SCALE = 3.0


def from_behind(value, axis, steps):
    count = lax.axis_size(axis)
    pairs = [(source, (source + steps) % count) for source in range(count)]
    return lax.ppermute(value, axis, pairs)


def body(states, premises, counts, partner_mask, send_rows, hard_idx):
    rows = states.shape[0]
    offer = send_rows.shape[2]
    loop_size = lax.axis_size("loop")
    group_size = lax.axis_size("groups")
    here = lax.axis_index("loop")
    group = lax.axis_index("groups")
    slots = jnp.arange(rows, dtype=jnp.int32)
    valid = slots < counts[0, 0]
    vflt = valid.astype(jnp.float32)
    partner = jnp.bitwise_xor(group, partner_mask[0])
    keys, counts_all = (
        lax.all_gather(premises, "loop", axis=0, tiled=True),
        lax.all_gather(counts, "loop", axis=0, tiled=True),
    )
    column = jnp.arange(loop_size * rows, dtype=jnp.int32)
    limits = jnp.repeat(counts_all[:, 0], rows)
    key_ok = column % rows < limits
    scores = SCALE * jnp.einsum("pd,kd->pk", states, keys, preferred_element_type=jnp.float32)
    masked = jnp.where(key_ok[None, :], scores, -jnp.inf)
    top = jnp.max(masked, axis=1)
    lse = top + jnp.log(jnp.sum(jnp.exp(masked - top[:, None]), axis=1))
    own_block = lax.dynamic_slice_in_dim(scores, here * rows, rows, 1)
    pos = jnp.diagonal(own_block)
    offered = premises[send_rows[0, 0]]
    piece = lax.all_gather(offered, "groups", axis=0, tiled=True)
    offset = partner * offer
    count = piece.shape[0]
    inside = jnp.logical_and(offset >= 0, offset < count)
    part = lax.dynamic_slice_in_dim(piece, jnp.clip(offset, 0, count - offer), offer, 0)
    pool = jnp.where(inside, part, jnp.zeros_like(offered))
    hard = pool[hard_idx]
    states_f = states.astype(jnp.float32)
    hard_f = hard.astype(jnp.float32)
    tval = SCALE * jnp.sum(states_f * hard_f, axis=-1)
    qval = jnp.where(valid, jax.nn.sigmoid(tval - pos), 0.0)
    terms = jnp.where(valid, lse - pos + jax.nn.softplus(tval - pos), 0.0)
    loss = lax.psum(jnp.sum(terms), ("loop", "groups")) / (loop_size * group_size * rows)
    prob = jnp.where(valid[:, None], jnp.exp(masked - lse[:, None]), 0.0).astype(jnp.bfloat16)
    dstate = jnp.dot(prob, keys, preferred_element_type=jnp.float32)
    grad_states = SCALE * (
        dstate + qval[:, None] * hard_f - (vflt + qval)[:, None] * premises.astype(jnp.float32)
    )

    def visit(step, carry):
        block = jnp.remainder(here - step, loop_size)
        columns = lax.dynamic_slice_in_dim(prob, block * rows, rows, 1)
        carry = carry + jnp.einsum("pk,pd->kd", columns, states, preferred_element_type=jnp.float32)
        return from_behind(carry.astype(jnp.bfloat16), "loop", 1).astype(carry.dtype)

    dprem = lax.fori_loop(0, loop_size, visit, jnp.zeros(states.shape, jnp.float32))
    pick = jax.nn.one_hot(hard_idx, offer, dtype=jnp.float32)
    back = SCALE * jnp.dot(pick.T, qval[:, None] * states_f, precision=lax.Precision.HIGHEST)
    piece = lax.all_gather(back, "groups", axis=0, tiled=True)
    offset = partner * offer
    count = piece.shape[0]
    inside = jnp.logical_and(offset >= 0, offset < count)
    part = lax.dynamic_slice_in_dim(piece, jnp.clip(offset, 0, count - offer), offer, 0)
    back_home = jnp.where(inside, part, jnp.zeros_like(back))
    place = jax.nn.one_hot(send_rows[0, 0], rows, dtype=jnp.float32)
    dhard = jnp.dot(place.T, back_home, precision=lax.Precision.HIGHEST)
    grad_premises = dprem - SCALE * (vflt + qval)[:, None] * states_f + dhard
    return (loss, grad_states.astype(jnp.bfloat16), grad_premises.astype(jnp.bfloat16))


def solution(mesh):
    return jax.shard_map(
        body,
        mesh=mesh,
        in_specs=(
            P(("loop", "groups"), None),
            P(("loop", "groups"), None),
            P("loop", "groups"),
            P("loop"),
            P("loop", "groups", None),
            P(("loop", "groups")),
        ),
        out_specs=(P(), P(("loop", "groups"), None), P(("loop", "groups"), None)),
        check_vma=False,
    )
```

profile of v0, /device:TPU:16, one launch (start us, length us, event | category | flops | bytes accessed | tf_op | source)
XLA Modules:
  0.0 425.0 jit_solution(1148805048968045579)
XLA Ops:
  7.9 2.2 gather_fusion.1
  14.2 12.4 %all-reduce = s32[16]{0:T(128)S(1)} all-reduce(s32[16]{0:T(128)S(1)} %bitcast_dynamic-update-slice_fusion), channel_id=1, replica_groups=mesh['loop'=16,'groups'=32] {'loop'}, use_global_device_ids=true, to_apply=%add | all-reduce | flops 16 | bytes 128
  27.4 71.7 %all-gather.9.cloned.1.call-done = bf16[512,1024]{1,0:T(8,128)(2,1)} async-done(((bf16[16,1024]{1,0:T(8,128)(2,1)}), bf16[512,1024]{1,0:T(8,128)(2,1)}) %all-gather.9.cloned.1.call-update) | async-done | bytes 1048592 | tf_op jit(solution)/shard_map/all_gather | solution.py:40
  102.0 38.2 %all-gather.5.cloned.1.call-done = bf16[2048,1024]{1,0:T(8,128)(2,1)} async-done(((bf16[128,1024]{1,0:T(8,128)(2,1)}), bf16[2048,1024]{1,0:T(8,128)(2,1)}) %all-gather.5.cloned.1.call-update) | async-done | bytes 4194320 | tf_op jit(solution)/shard_map/all_gather | solution.py:27
  140.1 3.9 select_reduce_fusion
  147.7 3.7 fusion.5
  151.4 100.6 %psum.7 = f32[]{:T(128)} all-reduce(f32[]{:T(128)} %get-tuple-element.170), channel_id=1, replica_groups=mesh['loop'=16,'groups'=32] {'loop','groups'}, use_global_device_ids=true, to_apply=%region_4.5 | all-reduce | flops 1 | bytes 8 | tf_op jit(solution)/shard_map/psum | solution.py:52
  252.7 162.5 %while.16 = (s32[]{:T(128)}, f32[128,1024]{1,0:T(8,128)S(1)}, s32[]{:T(128)}, bf16[128,2048]{1,0:T(8,128)(2,1)S(1)}, bf16[128,1024]{1,0:T(8,128)(2,1)S(1)}, /*in...) while((s32[]{:T(128)}, f32[128,1024]{1,0:T(8,128)S(1)}, ...), condition=%wide.region_6.7_spmd.clone, body=%wide.region_5.6_spmd.clone.sunk | while | flops 34078736 | bytes 2916682 | solution.py:65
  253.0 1.9 collective-permute-start
  254.9 7.9 %collective-permute-done = bf16[128,1024]{1,0:T(8,128)(2,1)S(1)} collective-permute-done((bf16[128,1024]{1,0:T(8,128)(2,1)S(1)}, bf16[128,1024]{1,0:T(8,128)(2,1)S(1)}, u32[]{:S(2)}, u32[]{:S(2)}) %collective-permute-start) | collective-permute-done | bytes 262176 | tf_op jit(solution)/shard_map/while/body/eval_jaxpr/ppermute | solution.py:12
  265.0 7.9 %collective-permute-done = bf16[128,1024]{1,0:T(8,128)(2,1)S(1)} collective-permute-done((bf16[128,1024]{1,0:T(8,128)(2,1)S(1)}, bf16[128,1024]{1,0:T(8,128)(2,1)S(1)}, u32[]{:S(2)}, u32[]{:S(2)}) %collective-permute-start) | collective-permute-done | bytes 262176 | tf_op jit(solution)/shard_map/while/body/eval_jaxpr/ppermute | solution.py:12
  273.3 1.9 collective-permute-start
  275.2 7.9 %collective-permute-done = bf16[128,1024]{1,0:T(8,128)(2,1)S(1)} collective-permute-done((bf16[128,1024]{1,0:T(8,128)(2,1)S(1)}, bf16[128,1024]{1,0:T(8,128)(2,1)S(1)}, u32[]{:S(2)}, u32[]{:S(2)}) %collective-permute-start) | collective-permute-done | bytes 262176 | tf_op jit(solution)/shard_map/while/body/eval_jaxpr/ppermute | solution.py:12
  283.4 1.9 collective-permute-start
  285.3 7.9 %collective-permute-done = bf16[128,1024]{1,0:T(8,128)(2,1)S(1)} collective-permute-done((bf16[128,1024]{1,0:T(8,128)(2,1)S(1)}, bf16[128,1024]{1,0:T(8,128)(2,1)S(1)}, u32[]{:S(2)}, u32[]{:S(2)}) %collective-permute-start) | collective-permute-done | bytes 262176 | tf_op jit(solution)/shard_map/while/body/eval_jaxpr/ppermute | solution.py:12
  293.6 1.9 collective-permute-start
  295.5 7.9 %collective-permute-done = bf16[128,1024]{1,0:T(8,128)(2,1)S(1)} collective-permute-done((bf16[128,1024]{1,0:T(8,128)(2,1)S(1)}, bf16[128,1024]{1,0:T(8,128)(2,1)S(1)}, u32[]{:S(2)}, u32[]{:S(2)}) %collective-permute-start) | collective-permute-done | bytes 262176 | tf_op jit(solution)/shard_map/while/body/eval_jaxpr/ppermute | solution.py:12
  305.7 7.9 %collective-permute-done = bf16[128,1024]{1,0:T(8,128)(2,1)S(1)} collective-permute-done((bf16[128,1024]{1,0:T(8,128)(2,1)S(1)}, bf16[128,1024]{1,0:T(8,128)(2,1)S(1)}, u32[]{:S(2)}, u32[]{:S(2)}) %collective-permute-start) | collective-permute-done | bytes 262176 | tf_op jit(solution)/shard_map/while/body/eval_jaxpr/ppermute | solution.py:12
  315.8 7.9 %collective-permute-done = bf16[128,1024]{1,0:T(8,128)(2,1)S(1)} collective-permute-done((bf16[128,1024]{1,0:T(8,128)(2,1)S(1)}, bf16[128,1024]{1,0:T(8,128)(2,1)S(1)}, u32[]{:S(2)}, u32[]{:S(2)}) %collective-permute-start) | collective-permute-done | bytes 262176 | tf_op jit(solution)/shard_map/while/body/eval_jaxpr/ppermute | solution.py:12
  326.0 7.9 %collective-permute-done = bf16[128,1024]{1,0:T(8,128)(2,1)S(1)} collective-permute-done((bf16[128,1024]{1,0:T(8,128)(2,1)S(1)}, bf16[128,1024]{1,0:T(8,128)(2,1)S(1)}, u32[]{:S(2)}, u32[]{:S(2)}) %collective-permute-start) | collective-permute-done | bytes 262176 | tf_op jit(solution)/shard_map/while/body/eval_jaxpr/ppermute | solution.py:12
  336.1 7.9 %collective-permute-done = bf16[128,1024]{1,0:T(8,128)(2,1)S(1)} collective-permute-done((bf16[128,1024]{1,0:T(8,128)(2,1)S(1)}, bf16[128,1024]{1,0:T(8,128)(2,1)S(1)}, u32[]{:S(2)}, u32[]{:S(2)}) %collective-permute-start) | collective-permute-done | bytes 262176 | tf_op jit(solution)/shard_map/while/body/eval_jaxpr/ppermute | solution.py:12
  346.3 7.9 %collective-permute-done = bf16[128,1024]{1,0:T(8,128)(2,1)S(1)} collective-permute-done((bf16[128,1024]{1,0:T(8,128)(2,1)S(1)}, bf16[128,1024]{1,0:T(8,128)(2,1)S(1)}, u32[]{:S(2)}, u32[]{:S(2)}) %collective-permute-start) | collective-permute-done | bytes 262176 | tf_op jit(solution)/shard_map/while/body/eval_jaxpr/ppermute | solution.py:12
  356.4 7.9 %collective-permute-done = bf16[128,1024]{1,0:T(8,128)(2,1)S(1)} collective-permute-done((bf16[128,1024]{1,0:T(8,128)(2,1)S(1)}, bf16[128,1024]{1,0:T(8,128)(2,1)S(1)}, u32[]{:S(2)}, u32[]{:S(2)}) %collective-permute-start) | collective-permute-done | bytes 262176 | tf_op jit(solution)/shard_map/while/body/eval_jaxpr/ppermute | solution.py:12
  364.7 1.9 collective-permute-start
  366.6 7.9 %collective-permute-done = bf16[128,1024]{1,0:T(8,128)(2,1)S(1)} collective-permute-done((bf16[128,1024]{1,0:T(8,128)(2,1)S(1)}, bf16[128,1024]{1,0:T(8,128)(2,1)S(1)}, u32[]{:S(2)}, u32[]{:S(2)}) %collective-permute-start) | collective-permute-done | bytes 262176 | tf_op jit(solution)/shard_map/while/body/eval_jaxpr/ppermute | solution.py:12
  376.7 7.9 %collective-permute-done = bf16[128,1024]{1,0:T(8,128)(2,1)S(1)} collective-permute-done((bf16[128,1024]{1,0:T(8,128)(2,1)S(1)}, bf16[128,1024]{1,0:T(8,128)(2,1)S(1)}, u32[]{:S(2)}, u32[]{:S(2)}) %collective-permute-start) | collective-permute-done | bytes 262176 | tf_op jit(solution)/shard_map/while/body/eval_jaxpr/ppermute | solution.py:12
  385.0 1.9 collective-permute-start
  386.9 7.9 %collective-permute-done = bf16[128,1024]{1,0:T(8,128)(2,1)S(1)} collective-permute-done((bf16[128,1024]{1,0:T(8,128)(2,1)S(1)}, bf16[128,1024]{1,0:T(8,128)(2,1)S(1)}, u32[]{:S(2)}, u32[]{:S(2)}) %collective-permute-start) | collective-permute-done | bytes 262176 | tf_op jit(solution)/shard_map/while/body/eval_jaxpr/ppermute | solution.py:12
  397.1 7.9 %collective-permute-done = bf16[128,1024]{1,0:T(8,128)(2,1)S(1)} collective-permute-done((bf16[128,1024]{1,0:T(8,128)(2,1)S(1)}, bf16[128,1024]{1,0:T(8,128)(2,1)S(1)}, u32[]{:S(2)}, u32[]{:S(2)}) %collective-permute-start) | collective-permute-done | bytes 262176 | tf_op jit(solution)/shard_map/while/body/eval_jaxpr/ppermute | solution.py:12
  405.3 1.9 collective-permute-start
  407.2 7.9 %collective-permute-done = bf16[128,1024]{1,0:T(8,128)(2,1)S(1)} collective-permute-done((bf16[128,1024]{1,0:T(8,128)(2,1)S(1)}, bf16[128,1024]{1,0:T(8,128)(2,1)S(1)}, u32[]{:S(2)}, u32[]{:S(2)}) %collective-permute-start) | collective-permute-done | bytes 262176 | tf_op jit(solution)/shard_map/while/body/eval_jaxpr/ppermute | solution.py:12
  415.2 2.1 fusion.6
  (76 shorter events, 32.8 us)
Async XLA Ops:
  7.2 91.9 %all-gather.9.cloned.1.call-start = ((), (), s32[]{:S(2)}) async-start(), calls=%async_computation.2 | async-start | bytes 1081344 | tf_op jit(solution)/shard_map/all_gather | solution.py:40
  10.1 130.0 %all-gather.5.cloned.1.call-start = ((), (), s32[]{:S(2)}) async-start(), calls=%async_computation | async-start | bytes 4456448 | tf_op jit(solution)/shard_map/all_gather | solution.py:27
  10.9 404.3 %all-gather.7.cloned.1.call-start = ((), (), s32[]{:S(2)}) async-start(), calls=%async_computation.1 | async-start | bytes 2162688 | tf_op jit(solution)/shard_map/all_gather | solution.py:68
  100.8 45.5 %copy-start = (bf16[128,1024]{1,0:T(8,128)(2,1)S(1)}, bf16[128,1024]{1,0:T(8,128)(2,1)}, u32[]{:S(2)}) copy-start(bf16[128,1024]{1,0:T(8,128)(2,1)} %param.8) | copy-start | bytes 786436
  100.8 45.5 %copy-start.2 = (s32[128]{0:T(128)S(1)}, s32[128]{0:T(128)}, u32[]{:S(2)}) copy-start(s32[128]{0:T(128)} %param.13) | copy-start | bytes 1540
  102.0 45.7 %copy-start.1 = (bf16[128,1024]{1,0:T(8,128)(2,1)S(1)}, bf16[128,1024]{1,0:T(8,128)(2,1)}, u32[]{:S(2)}) copy-start(bf16[128,1024]{1,0:T(8,128)(2,1)} %param.9) | copy-start | bytes 786436
  252.6 162.5 %copy-start.3 = (s32[1,1,16]{2,1,0:T(1,128)S(1)}, s32[1,1,16]{2,1,0:T(1,128)}, u32[]{:S(2)}) copy-start(s32[1,1,16]{2,1,0:T(1,128)} %param.12) | copy-start | bytes 196
  253.0 9.8 %collective-permute-start = (bf16[128,1024]{1,0:T(8,128)(2,1)S(1)}, bf16[128,1024]{1,0:T(8,128)(2,1)S(1)}, u32[]{:S(2)}, u32[]{:S(2)}) collective-permute-start(bf16[128,1024]{1,0:T(8,128)(2,1)S(1)} %fusion.36), channel_id=1, source_target_pairs={{0,32},{32,64},{64,96},{96,128},{128,160},{160,192},{192,224},{224... | collective-permute-start | bytes 786440 | tf_op jit(solution)/shard_map/while/body/eval_jaxpr/ppermute | solution.py:12
  263.1 9.8 %collective-permute-start = (bf16[128,1024]{1,0:T(8,128)(2,1)S(1)}, bf16[128,1024]{1,0:T(8,128)(2,1)S(1)}, u32[]{:S(2)}, u32[]{:S(2)}) collective-permute-start(bf16[128,1024]{1,0:T(8,128)(2,1)S(1)} %fusion.36), channel_id=1, source_target_pairs={{0,32},{32,64},{64,96},{96,128},{128,160},{160,192},{192,224},{224... | collective-permute-start | bytes 786440 | tf_op jit(solution)/shard_map/while/body/eval_jaxpr/ppermute | solution.py:12
  273.3 9.8 %collective-permute-start = (bf16[128,1024]{1,0:T(8,128)(2,1)S(1)}, bf16[128,1024]{1,0:T(8,128)(2,1)S(1)}, u32[]{:S(2)}, u32[]{:S(2)}) collective-permute-start(bf16[128,1024]{1,0:T(8,128)(2,1)S(1)} %fusion.36), channel_id=1, source_target_pairs={{0,32},{32,64},{64,96},{96,128},{128,160},{160,192},{192,224},{224... | collective-permute-start | bytes 786440 | tf_op jit(solution)/shard_map/while/body/eval_jaxpr/ppermute | solution.py:12
  283.4 9.8 %collective-permute-start = (bf16[128,1024]{1,0:T(8,128)(2,1)S(1)}, bf16[128,1024]{1,0:T(8,128)(2,1)S(1)}, u32[]{:S(2)}, u32[]{:S(2)}) collective-permute-start(bf16[128,1024]{1,0:T(8,128)(2,1)S(1)} %fusion.36), channel_id=1, source_target_pairs={{0,32},{32,64},{64,96},{96,128},{128,160},{160,192},{192,224},{224... | collective-permute-start | bytes 786440 | tf_op jit(solution)/shard_map/while/body/eval_jaxpr/ppermute | solution.py:12
  293.6 9.8 %collective-permute-start = (bf16[128,1024]{1,0:T(8,128)(2,1)S(1)}, bf16[128,1024]{1,0:T(8,128)(2,1)S(1)}, u32[]{:S(2)}, u32[]{:S(2)}) collective-permute-start(bf16[128,1024]{1,0:T(8,128)(2,1)S(1)} %fusion.36), channel_id=1, source_target_pairs={{0,32},{32,64},{64,96},{96,128},{128,160},{160,192},{192,224},{224... | collective-permute-start | bytes 786440 | tf_op jit(solution)/shard_map/while/body/eval_jaxpr/ppermute | solution.py:12
  303.7 9.8 %collective-permute-start = (bf16[128,1024]{1,0:T(8,128)(2,1)S(1)}, bf16[128,1024]{1,0:T(8,128)(2,1)S(1)}, u32[]{:S(2)}, u32[]{:S(2)}) collective-permute-start(bf16[128,1024]{1,0:T(8,128)(2,1)S(1)} %fusion.36), channel_id=1, source_target_pairs={{0,32},{32,64},{64,96},{96,128},{128,160},{160,192},{192,224},{224... | collective-permute-start | bytes 786440 | tf_op jit(solution)/shard_map/while/body/eval_jaxpr/ppermute | solution.py:12
  313.9 9.8 %collective-permute-start = (bf16[128,1024]{1,0:T(8,128)(2,1)S(1)}, bf16[128,1024]{1,0:T(8,128)(2,1)S(1)}, u32[]{:S(2)}, u32[]{:S(2)}) collective-permute-start(bf16[128,1024]{1,0:T(8,128)(2,1)S(1)} %fusion.36), channel_id=1, source_target_pairs={{0,32},{32,64},{64,96},{96,128},{128,160},{160,192},{192,224},{224... | collective-permute-start | bytes 786440 | tf_op jit(solution)/shard_map/while/body/eval_jaxpr/ppermute | solution.py:12
  324.0 9.8 %collective-permute-start = (bf16[128,1024]{1,0:T(8,128)(2,1)S(1)}, bf16[128,1024]{1,0:T(8,128)(2,1)S(1)}, u32[]{:S(2)}, u32[]{:S(2)}) collective-permute-start(bf16[128,1024]{1,0:T(8,128)(2,1)S(1)} %fusion.36), channel_id=1, source_target_pairs={{0,32},{32,64},{64,96},{96,128},{128,160},{160,192},{192,224},{224... | collective-permute-start | bytes 786440 | tf_op jit(solution)/shard_map/while/body/eval_jaxpr/ppermute | solution.py:12
  334.2 9.8 %collective-permute-start = (bf16[128,1024]{1,0:T(8,128)(2,1)S(1)}, bf16[128,1024]{1,0:T(8,128)(2,1)S(1)}, u32[]{:S(2)}, u32[]{:S(2)}) collective-permute-start(bf16[128,1024]{1,0:T(8,128)(2,1)S(1)} %fusion.36), channel_id=1, source_target_pairs={{0,32},{32,64},{64,96},{96,128},{128,160},{160,192},{192,224},{224... | collective-permute-start | bytes 786440 | tf_op jit(solution)/shard_map/while/body/eval_jaxpr/ppermute | solution.py:12
  344.4 9.8 %collective-permute-start = (bf16[128,1024]{1,0:T(8,128)(2,1)S(1)}, bf16[128,1024]{1,0:T(8,128)(2,1)S(1)}, u32[]{:S(2)}, u32[]{:S(2)}) collective-permute-start(bf16[128,1024]{1,0:T(8,128)(2,1)S(1)} %fusion.36), channel_id=1, source_target_pairs={{0,32},{32,64},{64,96},{96,128},{128,160},{160,192},{192,224},{224... | collective-permute-start | bytes 786440 | tf_op jit(solution)/shard_map/while/body/eval_jaxpr/ppermute | solution.py:12
  354.5 9.8 %collective-permute-start = (bf16[128,1024]{1,0:T(8,128)(2,1)S(1)}, bf16[128,1024]{1,0:T(8,128)(2,1)S(1)}, u32[]{:S(2)}, u32[]{:S(2)}) collective-permute-start(bf16[128,1024]{1,0:T(8,128)(2,1)S(1)} %fusion.36), channel_id=1, source_target_pairs={{0,32},{32,64},{64,96},{96,128},{128,160},{160,192},{192,224},{224... | collective-permute-start | bytes 786440 | tf_op jit(solution)/shard_map/while/body/eval_jaxpr/ppermute | solution.py:12
  364.7 9.8 %collective-permute-start = (bf16[128,1024]{1,0:T(8,128)(2,1)S(1)}, bf16[128,1024]{1,0:T(8,128)(2,1)S(1)}, u32[]{:S(2)}, u32[]{:S(2)}) collective-permute-start(bf16[128,1024]{1,0:T(8,128)(2,1)S(1)} %fusion.36), channel_id=1, source_target_pairs={{0,32},{32,64},{64,96},{96,128},{128,160},{160,192},{192,224},{224... | collective-permute-start | bytes 786440 | tf_op jit(solution)/shard_map/while/body/eval_jaxpr/ppermute | solution.py:12
  374.8 9.8 %collective-permute-start = (bf16[128,1024]{1,0:T(8,128)(2,1)S(1)}, bf16[128,1024]{1,0:T(8,128)(2,1)S(1)}, u32[]{:S(2)}, u32[]{:S(2)}) collective-permute-start(bf16[128,1024]{1,0:T(8,128)(2,1)S(1)} %fusion.36), channel_id=1, source_target_pairs={{0,32},{32,64},{64,96},{96,128},{128,160},{160,192},{192,224},{224... | collective-permute-start | bytes 786440 | tf_op jit(solution)/shard_map/while/body/eval_jaxpr/ppermute | solution.py:12
  385.0 9.8 %collective-permute-start = (bf16[128,1024]{1,0:T(8,128)(2,1)S(1)}, bf16[128,1024]{1,0:T(8,128)(2,1)S(1)}, u32[]{:S(2)}, u32[]{:S(2)}) collective-permute-start(bf16[128,1024]{1,0:T(8,128)(2,1)S(1)} %fusion.36), channel_id=1, source_target_pairs={{0,32},{32,64},{64,96},{96,128},{128,160},{160,192},{192,224},{224... | collective-permute-start | bytes 786440 | tf_op jit(solution)/shard_map/while/body/eval_jaxpr/ppermute | solution.py:12
  395.1 9.8 %collective-permute-start = (bf16[128,1024]{1,0:T(8,128)(2,1)S(1)}, bf16[128,1024]{1,0:T(8,128)(2,1)S(1)}, u32[]{:S(2)}, u32[]{:S(2)}) collective-permute-start(bf16[128,1024]{1,0:T(8,128)(2,1)S(1)} %fusion.36), channel_id=1, source_target_pairs={{0,32},{32,64},{64,96},{96,128},{128,160},{160,192},{192,224},{224... | collective-permute-start | bytes 786440 | tf_op jit(solution)/shard_map/while/body/eval_jaxpr/ppermute | solution.py:12
  405.3 9.8 %collective-permute-start = (bf16[128,1024]{1,0:T(8,128)(2,1)S(1)}, bf16[128,1024]{1,0:T(8,128)(2,1)S(1)}, u32[]{:S(2)}, u32[]{:S(2)}) collective-permute-start(bf16[128,1024]{1,0:T(8,128)(2,1)S(1)} %fusion.36), channel_id=1, source_target_pairs={{0,32},{32,64},{64,96},{96,128},{128,160},{160,192},{192,224},{224... | collective-permute-start | bytes 786440 | tf_op jit(solution)/shard_map/while/body/eval_jaxpr/ppermute | solution.py:12
Sparse Core Ops, SparseCore 0:
  11.7 87.3 all-gather.8
  101.2 38.8 all-gather.4
  147.5 86.5 all-gather.6
where the time goes:
time: 426 us; the launch traced here: 425 us
  waiting for transfers between devices  237 us (56%)
  blocking collectives  113 us (27%)
  starting transfers between devices  30.8 us (7%)
  between operations  17 us (4%)
  matrix products  14.9 us (3%)
  local copies, waits for them, and re-layouts  6.3 us (1%)
  other arithmetic  5.34 us (1%)
    ppermute x16, waiting for transfers between devices, from_behind(): return lax.ppermute(value, axis, pairs)  126 us
    psum x1, blocking collectives, body(): lax.psum(jnp.sum(terms), ('loop', 'groups'))  101 us
    all_gather x1, waiting for transfers between devices, body(): piece = lax.all_gather(offered, 'groups', axis=0, tiled=True)  71.7 us
    all_gather x1, waiting for transfers between devices, body(): lax.all_gather(premises, 'loop', axis=0, tiled=True)  38.2 us
    ppermute x16, starting transfers between devices, from_behind(): return lax.ppermute(value, axis, pairs)  30.7 us
    unnamed x1, blocking collectives  12.4 us
  transfers between devices with their start and end apart: 19, of which 18 were waited for; matrix products, arithmetic and copies ran while one was open for 3% of the time, Pallas kernels for 0%

commit v1 on v0

--- a/solution.py
+++ b/solution.py
@@ -4,6 +4,11 @@
 from jax.sharding import PartitionSpec as P
 
 SCALE = 3.0
+
+
+def swapped_in(shard, name, dim):
+    sent = jnp.stack([shard] * lax.axis_size(name))
+    return jnp.concatenate(lax.all_to_all(sent, name, 0, 0), axis=dim)
 
 
 def from_behind(value, axis, steps):
@@ -24,7 +29,7 @@
     vflt = valid.astype(jnp.float32)
     partner = jnp.bitwise_xor(group, partner_mask[0])
     keys, counts_all = (
-        lax.all_gather(premises, "loop", axis=0, tiled=True),
+        swapped_in(premises, "loop", 0),
         lax.all_gather(counts, "loop", axis=0, tiled=True),
     )
     column = jnp.arange(loop_size * rows, dtype=jnp.int32)

time: 426 us -> 392 us (0.920)
  waiting for transfers between devices: 237 us -> 161 us
  blocking collectives: 113 us -> 149 us
  starting transfers between devices: 30.8 us -> 36.4 us
    unnamed x1, blocking collectives: 12.4 us -> 51.9 us
    all_gather x1 -> x0, waiting for transfers between devices: 38.2 us -> none  [body(): lax.all_gather(premises, 'loop', axis=0, tiled=True)]
    all_gather x1, waiting for transfers between devices: 71.7 us -> 34.7 us  [body(): piece = lax.all_gather(offered, 'groups', axis=0, tiled=True)]
    all_to_all x0 -> x1, starting transfers between devices: none -> 5.61 us  [swapped_in(): return jnp.concatenate(lax.all_to_all(sent, name, 0, 0), axis=dim)]
  transfers between devices with their start and end apart: 19 -> 19, of which waited for: 18 -> 17; matrix products, arithmetic and copies ran while one was open for 3% -> 4% of each run, Pallas kernels for 0% -> 0%
where the time goes in v1:
time: 392 us; the launch traced here: 391 us
  waiting for transfers between devices  161 us (41%)
  blocking collectives  149 us (38%)
  starting transfers between devices  36.4 us (9%)
  between operations  17.3 us (4%)
  matrix products  14.9 us (4%)
  local copies, waits for them, and re-layouts  8.74 us (2%)
    ppermute x16, waiting for transfers between devices, from_behind(): return lax.ppermute(value, axis, pairs)  126 us
    psum x1, blocking collectives, body(): lax.psum(jnp.sum(terms), ('loop', 'groups'))  96.9 us
    unnamed x1, blocking collectives  51.9 us
    all_gather x1, waiting for transfers between devices, body(): piece = lax.all_gather(offered, 'groups', axis=0, tiled=True)  34.7 us
    ppermute x16, starting transfers between devices, from_behind(): return lax.ppermute(value, axis, pairs)  30.7 us
  transfers between devices with their start and end apart: 19, of which 17 were waited for; matrix products, arithmetic and copies ran while one was open for 4% of the time, Pallas kernels for 0%

profile of v1, /device:TPU:16, one launch (start us, length us, event | category | flops | bytes accessed | tf_op | source)
XLA Modules:
  0.0 390.8 jit_solution(3097697219827720423)
XLA Ops:
  7.2 3.5 stack.2
  10.6 5.6 %all-to-all-start = ((bf16[16,128,1024]{2,1,0:T(8,128)(2,1)}), bf16[16,128,1024]{2,1,0:T(8,128)(2,1)}, u32[]{:S(2)}, u32[]{:S(2)}) async-start(bf16[16,128,1024]{2,1,0:T(8,128)(2,1)} %stack.2), calls=%async_computation | async-start | bytes 8388608 | tf_op jit(solution)/shard_map/all_to_all | solution.py:11
  20.9 51.9 %all-reduce = s32[16]{0:T(128)S(1)} all-reduce(s32[16]{0:T(128)S(1)} %bitcast_dynamic-update-slice_fusion), channel_id=1, replica_groups=mesh['loop'=16,'groups'=32] {'loop'}, use_global_device_ids=true, to_apply=%add | all-reduce | flops 16 | bytes 128
  72.9 34.7 %all-gather.6.cloned.1.call-done = bf16[512,1024]{1,0:T(8,128)(2,1)} async-done(((bf16[16,1024]{1,0:T(8,128)(2,1)}), bf16[512,1024]{1,0:T(8,128)(2,1)}) %all-gather.6.cloned.1.call-update) | async-done | bytes 1048592 | tf_op jit(solution)/shard_map/all_gather | solution.py:45
  109.5 3.8 select_reduce_fusion
  116.9 3.7 fusion.5
  120.6 96.9 %psum.7 = f32[]{:T(128)} all-reduce(f32[]{:T(128)} %get-tuple-element.170), channel_id=1, replica_groups=mesh['loop'=16,'groups'=32] {'loop','groups'}, use_global_device_ids=true, to_apply=%region_4.5 | all-reduce | flops 1 | bytes 8 | tf_op jit(solution)/shard_map/psum | solution.py:57
  218.1 162.5 %while.16 = (s32[]{:T(128)}, f32[128,1024]{1,0:T(8,128)S(1)}, s32[]{:T(128)}, bf16[128,2048]{1,0:T(8,128)(2,1)S(1)}, bf16[128,1024]{1,0:T(8,128)(2,1)S(1)}, /*in...) while((s32[]{:T(128)}, f32[128,1024]{1,0:T(8,128)S(1)}, ...), condition=%wide.region_6.7_spmd.clone, body=%wide.region_5.6_spmd.clone.sunk | while | flops 34078736 | bytes 2916682 | solution.py:70
  218.5 1.9 collective-permute-start
  220.4 7.9 %collective-permute-done = bf16[128,1024]{1,0:T(8,128)(2,1)S(1)} collective-permute-done((bf16[128,1024]{1,0:T(8,128)(2,1)S(1)}, bf16[128,1024]{1,0:T(8,128)(2,1)S(1)}, u32[]{:S(2)}, u32[]{:S(2)}) %collective-permute-start) | collective-permute-done | bytes 262176 | tf_op jit(solution)/shard_map/while/body/eval_jaxpr/ppermute | solution.py:17
  228.6 1.9 collective-permute-start
  230.5 7.9 %collective-permute-done = bf16[128,1024]{1,0:T(8,128)(2,1)S(1)} collective-permute-done((bf16[128,1024]{1,0:T(8,128)(2,1)S(1)}, bf16[128,1024]{1,0:T(8,128)(2,1)S(1)}, u32[]{:S(2)}, u32[]{:S(2)}) %collective-permute-start) | collective-permute-done | bytes 262176 | tf_op jit(solution)/shard_map/while/body/eval_jaxpr/ppermute | solution.py:17
  238.8 1.9 collective-permute-start
  240.7 7.9 %collective-permute-done = bf16[128,1024]{1,0:T(8,128)(2,1)S(1)} collective-permute-done((bf16[128,1024]{1,0:T(8,128)(2,1)S(1)}, bf16[128,1024]{1,0:T(8,128)(2,1)S(1)}, u32[]{:S(2)}, u32[]{:S(2)}) %collective-permute-start) | collective-permute-done | bytes 262176 | tf_op jit(solution)/shard_map/while/body/eval_jaxpr/ppermute | solution.py:17
  250.8 7.9 %collective-permute-done = bf16[128,1024]{1,0:T(8,128)(2,1)S(1)} collective-permute-done((bf16[128,1024]{1,0:T(8,128)(2,1)S(1)}, bf16[128,1024]{1,0:T(8,128)(2,1)S(1)}, u32[]{:S(2)}, u32[]{:S(2)}) %collective-permute-start) | collective-permute-done | bytes 262176 | tf_op jit(solution)/shard_map/while/body/eval_jaxpr/ppermute | solution.py:17
  261.0 7.9 %collective-permute-done = bf16[128,1024]{1,0:T(8,128)(2,1)S(1)} collective-permute-done((bf16[128,1024]{1,0:T(8,128)(2,1)S(1)}, bf16[128,1024]{1,0:T(8,128)(2,1)S(1)}, u32[]{:S(2)}, u32[]{:S(2)}) %collective-permute-start) | collective-permute-done | bytes 262176 | tf_op jit(solution)/shard_map/while/body/eval_jaxpr/ppermute | solution.py:17
  271.1 7.9 %collective-permute-done = bf16[128,1024]{1,0:T(8,128)(2,1)S(1)} collective-permute-done((bf16[128,1024]{1,0:T(8,128)(2,1)S(1)}, bf16[128,1024]{1,0:T(8,128)(2,1)S(1)}, u32[]{:S(2)}, u32[]{:S(2)}) %collective-permute-start) | collective-permute-done | bytes 262176 | tf_op jit(solution)/shard_map/while/body/eval_jaxpr/ppermute | solution.py:17
  281.3 7.9 %collective-permute-done = bf16[128,1024]{1,0:T(8,128)(2,1)S(1)} collective-permute-done((bf16[128,1024]{1,0:T(8,128)(2,1)S(1)}, bf16[128,1024]{1,0:T(8,128)(2,1)S(1)}, u32[]{:S(2)}, u32[]{:S(2)}) %collective-permute-start) | collective-permute-done | bytes 262176 | tf_op jit(solution)/shard_map/while/body/eval_jaxpr/ppermute | solution.py:17
  291.5 7.9 %collective-permute-done = bf16[128,1024]{1,0:T(8,128)(2,1)S(1)} collective-permute-done((bf16[128,1024]{1,0:T(8,128)(2,1)S(1)}, bf16[128,1024]{1,0:T(8,128)(2,1)S(1)}, u32[]{:S(2)}, u32[]{:S(2)}) %collective-permute-start) | collective-permute-done | bytes 262176 | tf_op jit(solution)/shard_map/while/body/eval_jaxpr/ppermute | solution.py:17
  299.7 1.9 collective-permute-start
  301.6 7.9 %collective-permute-done = bf16[128,1024]{1,0:T(8,128)(2,1)S(1)} collective-permute-done((bf16[128,1024]{1,0:T(8,128)(2,1)S(1)}, bf16[128,1024]{1,0:T(8,128)(2,1)S(1)}, u32[]{:S(2)}, u32[]{:S(2)}) %collective-permute-start) | collective-permute-done | bytes 262176 | tf_op jit(solution)/shard_map/while/body/eval_jaxpr/ppermute | solution.py:17
  311.8 7.9 %collective-permute-done = bf16[128,1024]{1,0:T(8,128)(2,1)S(1)} collective-permute-done((bf16[128,1024]{1,0:T(8,128)(2,1)S(1)}, bf16[128,1024]{1,0:T(8,128)(2,1)S(1)}, u32[]{:S(2)}, u32[]{:S(2)}) %collective-permute-start) | collective-permute-done | bytes 262176 | tf_op jit(solution)/shard_map/while/body/eval_jaxpr/ppermute | solution.py:17
  321.9 7.9 %collective-permute-done = bf16[128,1024]{1,0:T(8,128)(2,1)S(1)} collective-permute-done((bf16[128,1024]{1,0:T(8,128)(2,1)S(1)}, bf16[128,1024]{1,0:T(8,128)(2,1)S(1)}, u32[]{:S(2)}, u32[]{:S(2)}) %collective-permute-start) | collective-permute-done | bytes 262176 | tf_op jit(solution)/shard_map/while/body/eval_jaxpr/ppermute | solution.py:17
  330.2 1.9 collective-permute-start
  332.1 7.9 %collective-permute-done = bf16[128,1024]{1,0:T(8,128)(2,1)S(1)} collective-permute-done((bf16[128,1024]{1,0:T(8,128)(2,1)S(1)}, bf16[128,1024]{1,0:T(8,128)(2,1)S(1)}, u32[]{:S(2)}, u32[]{:S(2)}) %collective-permute-start) | collective-permute-done | bytes 262176 | tf_op jit(solution)/shard_map/while/body/eval_jaxpr/ppermute | solution.py:17
  340.3 1.9 collective-permute-start
  342.2 7.9 %collective-permute-done = bf16[128,1024]{1,0:T(8,128)(2,1)S(1)} collective-permute-done((bf16[128,1024]{1,0:T(8,128)(2,1)S(1)}, bf16[128,1024]{1,0:T(8,128)(2,1)S(1)}, u32[]{:S(2)}, u32[]{:S(2)}) %collective-permute-start) | collective-permute-done | bytes 262176 | tf_op jit(solution)/shard_map/while/body/eval_jaxpr/ppermute | solution.py:17
  352.4 7.9 %collective-permute-done = bf16[128,1024]{1,0:T(8,128)(2,1)S(1)} collective-permute-done((bf16[128,1024]{1,0:T(8,128)(2,1)S(1)}, bf16[128,1024]{1,0:T(8,128)(2,1)S(1)}, u32[]{:S(2)}, u32[]{:S(2)}) %collective-permute-start) | collective-permute-done | bytes 262176 | tf_op jit(solution)/shard_map/while/body/eval_jaxpr/ppermute | solution.py:17
  360.6 1.9 collective-permute-start
  362.6 7.9 %collective-permute-done = bf16[128,1024]{1,0:T(8,128)(2,1)S(1)} collective-permute-done((bf16[128,1024]{1,0:T(8,128)(2,1)S(1)}, bf16[128,1024]{1,0:T(8,128)(2,1)S(1)}, u32[]{:S(2)}, u32[]{:S(2)}) %collective-permute-start) | collective-permute-done | bytes 262176 | tf_op jit(solution)/shard_map/while/body/eval_jaxpr/ppermute | solution.py:17
  372.7 7.9 %collective-permute-done = bf16[128,1024]{1,0:T(8,128)(2,1)S(1)} collective-permute-done((bf16[128,1024]{1,0:T(8,128)(2,1)S(1)}, bf16[128,1024]{1,0:T(8,128)(2,1)S(1)}, u32[]{:S(2)}, u32[]{:S(2)}) %collective-permute-start) | collective-permute-done | bytes 262176 | tf_op jit(solution)/shard_map/while/body/eval_jaxpr/ppermute | solution.py:17
  380.7 2.1 fusion.6
  (76 shorter events, 30.9 us)
Async XLA Ops:
  10.6 5.7 %copy-start.3 = (s32[1,1,16]{2,1,0:T(1,128)S(1)}, s32[1,1,16]{2,1,0:T(1,128)}, u32[]{:S(2)}) copy-start(s32[1,1,16]{2,1,0:T(1,128)} %param.12) | copy-start | bytes 196
  10.6 5.7 %copy-start.1 = (bf16[128,1024]{1,0:T(8,128)(2,1)S(1)}, bf16[128,1024]{1,0:T(8,128)(2,1)}, u32[]{:S(2)}) copy-start(bf16[128,1024]{1,0:T(8,128)(2,1)} %param.9) | copy-start | bytes 786436
  10.6 62.2 %copy-start.2 = (s32[128]{0:T(128)S(1)}, s32[128]{0:T(128)}, u32[]{:S(2)}) copy-start(s32[128]{0:T(128)} %param.13) | copy-start | bytes 1540
  10.6 98.7 %copy-start = (bf16[128,1024]{1,0:T(8,128)(2,1)S(1)}, bf16[128,1024]{1,0:T(8,128)(2,1)}, u32[]{:S(2)}) copy-start(bf16[128,1024]{1,0:T(8,128)(2,1)} %param.8) | copy-start | bytes 786436
  10.6 98.9 %all-to-all-start = ((bf16[16,128,1024]{2,1,0:T(8,128)(2,1)}), bf16[16,128,1024]{2,1,0:T(8,128)(2,1)}, u32[]{:S(2)}, u32[]{:S(2)}) async-start(bf16[16,128,1024]{2,1,0:T(8,128)(2,1)} %stack.2), calls=%async_computation | async-start | bytes 8388608 | tf_op jit(solution)/shard_map/all_to_all | solution.py:11
  16.2 91.4 %all-gather.6.cloned.1.call-start = ((), (), s32[]{:S(2)}) async-start(), calls=%async_computation.2 | async-start | bytes 1081344 | tf_op jit(solution)/shard_map/all_gather | solution.py:45
  17.6 363.1 %all-gather.4.cloned.1.call-start = ((), (), s32[]{:S(2)}) async-start(), calls=%async_computation.1 | async-start | bytes 2162688 | tf_op jit(solution)/shard_map/all_gather | solution.py:73
  218.5 9.8 %collective-permute-start = (bf16[128,1024]{1,0:T(8,128)(2,1)S(1)}, bf16[128,1024]{1,0:T(8,128)(2,1)S(1)}, u32[]{:S(2)}, u32[]{:S(2)}) collective-permute-start(bf16[128,1024]{1,0:T(8,128)(2,1)S(1)} %fusion.36), channel_id=1, source_target_pairs={{0,32},{32,64},{64,96},{96,128},{128,160},{160,192},{192,224},{224... | collective-permute-start | bytes 786440 | tf_op jit(solution)/shard_map/while/body/eval_jaxpr/ppermute | solution.py:17
  228.6 9.8 %collective-permute-start = (bf16[128,1024]{1,0:T(8,128)(2,1)S(1)}, bf16[128,1024]{1,0:T(8,128)(2,1)S(1)}, u32[]{:S(2)}, u32[]{:S(2)}) collective-permute-start(bf16[128,1024]{1,0:T(8,128)(2,1)S(1)} %fusion.36), channel_id=1, source_target_pairs={{0,32},{32,64},{64,96},{96,128},{128,160},{160,192},{192,224},{224... | collective-permute-start | bytes 786440 | tf_op jit(solution)/shard_map/while/body/eval_jaxpr/ppermute | solution.py:17
  238.8 9.8 %collective-permute-start = (bf16[128,1024]{1,0:T(8,128)(2,1)S(1)}, bf16[128,1024]{1,0:T(8,128)(2,1)S(1)}, u32[]{:S(2)}, u32[]{:S(2)}) collective-permute-start(bf16[128,1024]{1,0:T(8,128)(2,1)S(1)} %fusion.36), channel_id=1, source_target_pairs={{0,32},{32,64},{64,96},{96,128},{128,160},{160,192},{192,224},{224... | collective-permute-start | bytes 786440 | tf_op jit(solution)/shard_map/while/body/eval_jaxpr/ppermute | solution.py:17
  248.9 9.8 %collective-permute-start = (bf16[128,1024]{1,0:T(8,128)(2,1)S(1)}, bf16[128,1024]{1,0:T(8,128)(2,1)S(1)}, u32[]{:S(2)}, u32[]{:S(2)}) collective-permute-start(bf16[128,1024]{1,0:T(8,128)(2,1)S(1)} %fusion.36), channel_id=1, source_target_pairs={{0,32},{32,64},{64,96},{96,128},{128,160},{160,192},{192,224},{224... | collective-permute-start | bytes 786440 | tf_op jit(solution)/shard_map/while/body/eval_jaxpr/ppermute | solution.py:17
  259.1 9.8 %collective-permute-start = (bf16[128,1024]{1,0:T(8,128)(2,1)S(1)}, bf16[128,1024]{1,0:T(8,128)(2,1)S(1)}, u32[]{:S(2)}, u32[]{:S(2)}) collective-permute-start(bf16[128,1024]{1,0:T(8,128)(2,1)S(1)} %fusion.36), channel_id=1, source_target_pairs={{0,32},{32,64},{64,96},{96,128},{128,160},{160,192},{192,224},{224... | collective-permute-start | bytes 786440 | tf_op jit(solution)/shard_map/while/body/eval_jaxpr/ppermute | solution.py:17
  269.2 9.8 %collective-permute-start = (bf16[128,1024]{1,0:T(8,128)(2,1)S(1)}, bf16[128,1024]{1,0:T(8,128)(2,1)S(1)}, u32[]{:S(2)}, u32[]{:S(2)}) collective-permute-start(bf16[128,1024]{1,0:T(8,128)(2,1)S(1)} %fusion.36), channel_id=1, source_target_pairs={{0,32},{32,64},{64,96},{96,128},{128,160},{160,192},{192,224},{224... | collective-permute-start | bytes 786440 | tf_op jit(solution)/shard_map/while/body/eval_jaxpr/ppermute | solution.py:17
  279.4 9.8 %collective-permute-start = (bf16[128,1024]{1,0:T(8,128)(2,1)S(1)}, bf16[128,1024]{1,0:T(8,128)(2,1)S(1)}, u32[]{:S(2)}, u32[]{:S(2)}) collective-permute-start(bf16[128,1024]{1,0:T(8,128)(2,1)S(1)} %fusion.36), channel_id=1, source_target_pairs={{0,32},{32,64},{64,96},{96,128},{128,160},{160,192},{192,224},{224... | collective-permute-start | bytes 786440 | tf_op jit(solution)/shard_map/while/body/eval_jaxpr/ppermute | solution.py:17
  289.5 9.8 %collective-permute-start = (bf16[128,1024]{1,0:T(8,128)(2,1)S(1)}, bf16[128,1024]{1,0:T(8,128)(2,1)S(1)}, u32[]{:S(2)}, u32[]{:S(2)}) collective-permute-start(bf16[128,1024]{1,0:T(8,128)(2,1)S(1)} %fusion.36), channel_id=1, source_target_pairs={{0,32},{32,64},{64,96},{96,128},{128,160},{160,192},{192,224},{224... | collective-permute-start | bytes 786440 | tf_op jit(solution)/shard_map/while/body/eval_jaxpr/ppermute | solution.py:17
  299.7 9.8 %collective-permute-start = (bf16[128,1024]{1,0:T(8,128)(2,1)S(1)}, bf16[128,1024]{1,0:T(8,128)(2,1)S(1)}, u32[]{:S(2)}, u32[]{:S(2)}) collective-permute-start(bf16[128,1024]{1,0:T(8,128)(2,1)S(1)} %fusion.36), channel_id=1, source_target_pairs={{0,32},{32,64},{64,96},{96,128},{128,160},{160,192},{192,224},{224... | collective-permute-start | bytes 786440 | tf_op jit(solution)/shard_map/while/body/eval_jaxpr/ppermute | solution.py:17
  309.8 9.8 %collective-permute-start = (bf16[128,1024]{1,0:T(8,128)(2,1)S(1)}, bf16[128,1024]{1,0:T(8,128)(2,1)S(1)}, u32[]{:S(2)}, u32[]{:S(2)}) collective-permute-start(bf16[128,1024]{1,0:T(8,128)(2,1)S(1)} %fusion.36), channel_id=1, source_target_pairs={{0,32},{32,64},{64,96},{96,128},{128,160},{160,192},{192,224},{224... | collective-permute-start | bytes 786440 | tf_op jit(solution)/shard_map/while/body/eval_jaxpr/ppermute | solution.py:17
  320.0 9.8 %collective-permute-start = (bf16[128,1024]{1,0:T(8,128)(2,1)S(1)}, bf16[128,1024]{1,0:T(8,128)(2,1)S(1)}, u32[]{:S(2)}, u32[]{:S(2)}) collective-permute-start(bf16[128,1024]{1,0:T(8,128)(2,1)S(1)} %fusion.36), channel_id=1, source_target_pairs={{0,32},{32,64},{64,96},{96,128},{128,160},{160,192},{192,224},{224... | collective-permute-start | bytes 786440 | tf_op jit(solution)/shard_map/while/body/eval_jaxpr/ppermute | solution.py:17
  330.2 9.8 %collective-permute-start = (bf16[128,1024]{1,0:T(8,128)(2,1)S(1)}, bf16[128,1024]{1,0:T(8,128)(2,1)S(1)}, u32[]{:S(2)}, u32[]{:S(2)}) collective-permute-start(bf16[128,1024]{1,0:T(8,128)(2,1)S(1)} %fusion.36), channel_id=1, source_target_pairs={{0,32},{32,64},{64,96},{96,128},{128,160},{160,192},{192,224},{224... | collective-permute-start | bytes 786440 | tf_op jit(solution)/shard_map/while/body/eval_jaxpr/ppermute | solution.py:17
  340.3 9.8 %collective-permute-start = (bf16[128,1024]{1,0:T(8,128)(2,1)S(1)}, bf16[128,1024]{1,0:T(8,128)(2,1)S(1)}, u32[]{:S(2)}, u32[]{:S(2)}) collective-permute-start(bf16[128,1024]{1,0:T(8,128)(2,1)S(1)} %fusion.36), channel_id=1, source_target_pairs={{0,32},{32,64},{64,96},{96,128},{128,160},{160,192},{192,224},{224... | collective-permute-start | bytes 786440 | tf_op jit(solution)/shard_map/while/body/eval_jaxpr/ppermute | solution.py:17
  350.5 9.8 %collective-permute-start = (bf16[128,1024]{1,0:T(8,128)(2,1)S(1)}, bf16[128,1024]{1,0:T(8,128)(2,1)S(1)}, u32[]{:S(2)}, u32[]{:S(2)}) collective-permute-start(bf16[128,1024]{1,0:T(8,128)(2,1)S(1)} %fusion.36), channel_id=1, source_target_pairs={{0,32},{32,64},{64,96},{96,128},{128,160},{160,192},{192,224},{224... | collective-permute-start | bytes 786440 | tf_op jit(solution)/shard_map/while/body/eval_jaxpr/ppermute | solution.py:17
  360.6 9.8 %collective-permute-start = (bf16[128,1024]{1,0:T(8,128)(2,1)S(1)}, bf16[128,1024]{1,0:T(8,128)(2,1)S(1)}, u32[]{:S(2)}, u32[]{:S(2)}) collective-permute-start(bf16[128,1024]{1,0:T(8,128)(2,1)S(1)} %fusion.36), channel_id=1, source_target_pairs={{0,32},{32,64},{64,96},{96,128},{128,160},{160,192},{192,224},{224... | collective-permute-start | bytes 786440 | tf_op jit(solution)/shard_map/while/body/eval_jaxpr/ppermute | solution.py:17
  370.8 9.8 %collective-permute-start = (bf16[128,1024]{1,0:T(8,128)(2,1)S(1)}, bf16[128,1024]{1,0:T(8,128)(2,1)S(1)}, u32[]{:S(2)}, u32[]{:S(2)}) collective-permute-start(bf16[128,1024]{1,0:T(8,128)(2,1)S(1)} %fusion.36), channel_id=1, source_target_pairs={{0,32},{32,64},{64,96},{96,128},{128,160},{160,192},{192,224},{224... | collective-permute-start | bytes 786440 | tf_op jit(solution)/shard_map/while/body/eval_jaxpr/ppermute | solution.py:17
Sparse Core Ops, SparseCore 0:
  20.8 86.7 all-gather.5
  116.7 82.5 all-gather.3
